TPU v7x, 256 devices: a whole 4x4x8 slice. The times are simulated.
256 devices in a mesh: seq: 64 (over z, y, core), head: 4 (over x).
Axes of the slice: x: 4, y: 4, z: 8, core: 2. Of those that a mesh axis runs over, the one named last changes fastest.
Arguments:
- queries: bfloat16 [32, 64, 128], P(None, 'head'), may hold values from -12 to 12
- keys: bfloat16 [32, 8, 8192, 128], P(None, 'head', 'seq'), may hold values from -6 to 6
- values: bfloat16 [32, 8, 8192, 128], P(None, 'head', 'seq'), may hold values from -6 to 6
- codes: int32 [32, 8, 32, 8192], P(None, 'head', None, 'seq'), may hold values from 0 to 255
- centroids: float32 [8, 4, 32, 256], P('head'), may hold values from -6 to 6
- picks: int32 [32, 8, 64], P(None, 'head'), may hold values from 0 to 511, as said below
- block_len: int32 [32, 512], P(None, 'seq'), may hold values from 1 to 16
- out_weight: bfloat16 [8192, 8192], P('head', 'seq'), may hold values from -0.0625 to 0.0625
Outputs:
- estimates: float32 [32, 8, 512], P(None, 'head', 'seq')
- attended: bfloat16 [64, 4, 1024], P('seq', 'head')
- layer_out: bfloat16 [32, 8192], P('head', 'seq')
Inputs may be any that keep to these rules, and one draw needn't show every extreme that they name: Each row picks[b, h, :] holds 64 different block numbers in no particular order; among the 8 blocks j * 8 to (j + 1) * 8 - 1 of any j at most 4 are picked, and in every row some j has exactly 4.
All inputs are finite; a program needn't handle non-finite values.
Results may differ from a plain program's by a relative error of at most 0.0049.
Values may be sent and summed in bfloat16 or wider, within the bound.
A program may use at most 64 MiB of HBM per device.

v0:
```python
import jax
import jax.numpy as jnp
from jax import lax
from jax.sharding import PartitionSpec as P

NEG = -1e30


def slot_matrix(sel_rows, shard, nblk_dev, capacity):
    local = sel_rows - shard * nblk_dev
    inside = (local >= 0) & (local < nblk_dev)
    hits = (local[:, :, None] == lax.iota(jnp.int32, nblk_dev)[None, None, :]) & inside[:, :, None]
    taken = jnp.sum(hits.astype(jnp.int32), axis=1)
    position = jnp.cumsum(taken, axis=1) - 1
    place = (position[:, None, :] == lax.iota(jnp.int32, capacity)[None, :, None]) & (
        taken[:, None, :] > 0
    )
    return place.astype(jnp.bfloat16)


def attend(query, keys_s, values_s, lens_s):
    pairs, rows, width = keys_s.shape
    head_dim = query.shape[-1]
    block = width // head_dim
    key_rows = keys_s.reshape(pairs, rows * block, head_dim)
    value_rows = values_s.reshape(pairs, rows * block, head_dim)
    score = jnp.einsum(
        "pgd,ptd->pgt", query, key_rows, preferred_element_type=jnp.float32
    ) * head_dim ** (-0.5)
    live = (
        lax.iota(jnp.int32, block).astype(jnp.float32)[None, None, :]
        < lens_s.astype(jnp.float32)[:, :, None]
    )
    live = live.reshape(pairs, 1, rows * block)
    top = jnp.max(jnp.where(live, score, NEG), axis=2)
    weight = jnp.where(live, jnp.exp(score - top[:, :, None]), 0.0)
    total = jnp.sum(weight, axis=2)
    acc = jnp.einsum(
        "pgt,ptd->pgd", weight, value_rows.astype(jnp.float32), precision=lax.Precision.HIGHEST
    )
    return (top, total, acc)


def fold_rows(top, total, acc):
    best = jnp.max(top, axis=0)
    scale = jnp.exp(top - best[None])
    return (best, jnp.sum(total * scale, axis=0), jnp.sum(acc * scale[..., None], axis=0))


def shards(queries, keys, values, codes, centroids, picks, block_len, out_weight):
    batch, kv_local, seq_local, head_dim = keys.shape
    group = queries.shape[1] // kv_local
    nblk_dev = block_len.shape[1]
    block = seq_local // nblk_dev
    capacity = nblk_dev // 2
    pairs = batch * kv_local
    sub = centroids.shape[1]
    nsub = centroids.shape[2]
    cent = centroids.shape[3]
    shard = lax.axis_index("seq")
    query_float = queries.astype(jnp.float32).reshape(batch, kv_local, group, nsub, sub)
    table = jnp.einsum(
        "bhgms,hsmc->bhgmc", query_float, centroids, precision=lax.Precision.HIGHEST
    ) * head_dim ** (-0.5)
    table = table.astype(jnp.bfloat16).reshape(pairs, group, nsub * cent)
    lens_pair = jnp.repeat(block_len, kv_local, axis=0)
    step_rows = 4
    steps_count = pairs // step_rows

    def score_group(carry, items):
        tab, code, lens = items
        onehot = (code[:, :, None, :] == lax.iota(jnp.int32, cent)[None, None, :, None]).astype(
            jnp.bfloat16
        )
        onehot = onehot.reshape(step_rows, nsub * cent, seq_local)
        approx = jnp.einsum("pgk,pkt->pgt", tab, onehot, preferred_element_type=jnp.float32)
        approx = approx.reshape(step_rows, group, nblk_dev, block)
        live = (lax.iota(jnp.int32, block)[None, None, :] < lens[:, :, None])[:, None]
        top = jnp.max(jnp.where(live, approx, NEG), axis=(1, 3))
        mass = jnp.sum(jnp.where(live, jnp.exp(approx - top[:, None, :, None]), 0.0), axis=(1, 3))
        return (carry, top + jnp.log(mass))

    grouped = (
        table.reshape(steps_count, step_rows, group, nsub * cent),
        codes.reshape(steps_count, step_rows, nsub, seq_local),
        lens_pair.reshape(steps_count, step_rows, nblk_dev),
    )
    unused, estimated = lax.scan(score_group, 0, grouped)
    estimates = estimated.reshape(batch, kv_local, nblk_dev)
    sel_rows = picks.reshape(pairs, picks.shape[-1])
    place = slot_matrix(sel_rows, shard, nblk_dev, capacity)
    key_blocks = keys.reshape(pairs, nblk_dev, block * head_dim)
    value_blocks = values.reshape(pairs, nblk_dev, block * head_dim)
    lens_float = lens_pair.astype(jnp.float32)
    query_all = queries.reshape(pairs, group, head_dim)
    own_query = lax.dynamic_slice_in_dim(query_all, shard, 1, 0)
    send_keys = jnp.einsum(
        "pcn,pnd->cpd", place, key_blocks, preferred_element_type=jnp.float32
    ).astype(jnp.bfloat16)
    send_values = jnp.einsum(
        "pcn,pnd->cpd", place, value_blocks, preferred_element_type=jnp.float32
    ).astype(jnp.bfloat16)
    send_lens = jnp.einsum("pcn,pn->cp", place.astype(jnp.float32), lens_float).astype(jnp.bfloat16)
    got_keys = lax.all_to_all(send_keys, "seq", split_axis=1, concat_axis=1, tiled=True)
    got_values = lax.all_to_all(send_values, "seq", split_axis=1, concat_axis=1, tiled=True)
    got_lens = lax.all_to_all(send_lens, "seq", split_axis=1, concat_axis=1, tiled=True)
    count = got_keys.shape[0]
    query_rep = jnp.broadcast_to(own_query, (count, group, head_dim))
    pieces = attend(query_rep, got_keys, got_values, got_lens)
    top, total, acc = fold_rows(pieces[0], pieces[1], pieces[2])
    head_out = (acc / total[..., None]).astype(jnp.bfloat16)
    attended = head_out.reshape(1, 1, group * head_dim)
    flat = head_out.reshape(1, group * head_dim)
    weight_parts = out_weight.reshape(kv_local, group * head_dim, out_weight.shape[1])
    piece = lax.all_gather(flat, "seq", axis=0, tiled=True)
    products = jnp.einsum("ik,hkd->ihd", piece, weight_parts, preferred_element_type=jnp.float32)
    parity = lax.iota(jnp.int32, piece.shape[0]) % kv_local
    select = (parity[:, None] == lax.iota(jnp.int32, kv_local)[None, :]).astype(jnp.float32)
    gathered = jnp.sum(products * select[:, :, None], axis=1)
    per_request = jnp.sum(gathered.reshape(batch, kv_local, out_weight.shape[1]), axis=1)
    layer_out = lax.psum_scatter(per_request, "head", scatter_dimension=0, tiled=True).astype(
        jnp.bfloat16
    )
    return (estimates, attended, layer_out)


def solution(mesh):
    placed = (
        P(None, "head", None),
        P(None, "head", "seq", None),
        P(None, "head", "seq", None),
        P(None, "head", None, "seq"),
        P("head", None, None, None),
        P(None, "head", None),
        P(None, "seq"),
        P("head", "seq"),
    )
    return jax.shard_map(
        shards,
        mesh=mesh,
        in_specs=placed,
        out_specs=(P(None, "head", "seq"), P("seq", "head", None), P("head", "seq")),
        check_vma=False,
    )
```

profile of v0, /device:TPU:1, one launch (start us, length us, event | category | flops | bytes accessed | tf_op | source)
XLA Modules:
  0.0 275.0 jit_solution(5679206314056601219)
XLA Ops:
  4.7 13.1 %all-to-all-start = ((bf16[4,64,1]{0,2,1:T(2,128)(2,1)}), bf16[4,64,1]{0,2,1:T(2,128)(2,1)S(1)}, u32[]{:S(2)}, u32[]{:S(2)}) async-start(bf16[4,64,1]{0,2,1:T(2,128)(2,1)} %copy.64), calls=%async_computation | async-start | bytes 65536 | tf_op jit(solution)/shard_map/all_to_all | solution.py:106
  17.9 2.8 %reshape.221 = bf16[64,8,2048]{2,1,0:T(8,128)(2,1)S(1)} reshape(bf16[32,2,128,128]{3,2,1,0:T(8,128)(2,1)} %param.11) | data formatting | bytes 4194304 | tf_op jit(solution)/shard_map/reshape | solution.py:92
  20.7 1.7 fusion.5
  22.5 4.8 %all-to-all-done = bf16[4,64,1]{0,2,1:T(2,128)(2,1)S(1)} async-done(((bf16[4,64,1]{0,2,1:T(2,128)(2,1)}), bf16[4,64,1]{0,2,1:T(2,128)(2,1)S(1)}, u32[]{:S(2)}, u32[]{:S(2)}) %all-to-all-start) | async-done | bytes 544 | tf_op jit(solution)/shard_map/all_to_all | solution.py:106
  27.3 5.8 %all-to-all-start.1 = ((bf16[4,64,2048]{2,0,1:T(4,128)(2,1)}), bf16[4,64,2048]{2,0,1:T(4,128)(2,1)}, u32[]{:S(2)}, u32[]{:S(2)}) async-start(bf16[4,64,2048]{2,0,1:T(4,128)(2,1)} %fusion.5), calls=%async_computation.1 | async-start | bytes 2097152 | tf_op jit(solution)/shard_map/all_to_all | solution.py:104
  33.2 2.8 %reshape.223 = bf16[64,8,2048]{2,1,0:T(8,128)(2,1)S(1)} reshape(bf16[32,2,128,128]{3,2,1,0:T(8,128)(2,1)} %param.12) | data formatting | bytes 4194304 | tf_op jit(solution)/shard_map/reshape | solution.py:93
  37.5 9.1 %fusion.4 = bf16[32,2,8,32,256]{4,0,2,3,1:T(8,128)(2,1)} fusion(bf16[32,2,8,32,4]{0,2,1,4,3:T(8,128)(2,1)S(1)} %bitcast.87, f32[2,4,32,256,1]{3,2,1,0,4:T(8,128)S(1)} %bitcast.90), kind=kOutput, calls=%fused_computation.13 | convolution fusion | flops 209715200 | bytes 8781824 | tf_op jit(solution)/shard_map/bhgms,hsmc->bhgmc/dot_general | solution.py:62
  46.6 11.4 %copy.62 = bf16[32,2,8,32,256]{4,3,2,1,0:T(8,128)(2,1)} copy(bf16[32,2,8,32,256]{4,0,2,3,1:T(8,128)(2,1)} %fusion.4) | data formatting | bytes 16777216 | tf_op jit(solution)/shard_map/convert_element_type | solution.py:65
  57.9 13.5 %reshape_reshape.7 = bf16[16,4,8,8192]{3,2,1,0:T(8,128)(2,1)} reshape(bf16[32,2,8,32,256]{4,3,2,1,0:T(8,128)(2,1)} %copy.62) | data formatting | bytes 16777216 | tf_op jit(solution)/shard_map/reshape;reshape | solution.py:84
  71.4 1.8 fusion.6
  73.2 10.3 %all-to-all-start.2 = ((bf16[4,64,2048]{2,0,1:T(4,128)(2,1)}), bf16[4,64,2048]{2,0,1:T(4,128)(2,1)S(1)}, u32[]{:S(2)}, u32[]{:S(2)}) async-start(bf16[4,64,2048]{2,0,1:T(4,128)(2,1)} %fusion.6), calls=%async_computation.2 | async-start | bytes 2097152 | tf_op jit(solution)/shard_map/all_to_all | solution.py:105
  83.5 120.3 %while.10 = (s32[]{:T(128)}, f32[16,4,8]{2,1,0:T(4,128)S(1)}, s32[16,4,8]{2,1,0:T(4,128)S(1)}, bf16[16,4,8,8192]{3,2,1,0:T(8,128)(2,1)}, s32[16,4,32,128]{3,2,1,0:T(8,128)}, /*index=5*/s32[]{:T(128)}, f32[]{:T(128)}, f32[]{:T(128)}) while((s32[]{:T(128)}, f32[16,4,8]{2,1,0:T(4,128)S(1)}, s32[16,4,8]{2,1,0:T(4,128)S(1)}, ...), condition=%wide.region_5.6_spmd, body=%wide.region_0.5_spmd.sunk | while | flops 71324128 | bytes 9317225 | solution.py:88
  84.7 2.7 bitcast_compare_fusion.2
  87.4 3.1 %select_reduce_fusion.6 = (f32[4,128]{1,0:T(4,128)S(1)}, f32[4,8,128]{2,1,0:T(8,128)S(1)}) fusion(pred[4,128]{1,0:T(4,128)(4,1)S(1)} %broadcast_compare_fusion.4, pred[4,8192,128]{2,1,0:T(32,128)(4,1)S(1)} %bitcast_compare_fusion.2, bf16[16,4,8,8192]{3,2,1,0:T(8,128)(2,1)} %get-tuple-element.121, s32[]{:T(128)} %get-tuple-element.110), kind=kOutput, calls=%fused_computation.7.clone.1 | convolution fusion | flops 67116544 | bytes 4738048 | tf_op jit(solution)/shard_map/while/body/eval_jaxpr/pgk,pkt->pgt/dot_general | solution.py:76
  92.2 2.7 bitcast_compare_fusion.2
  94.9 3.1 %select_reduce_fusion.6 = (f32[4,128]{1,0:T(4,128)S(1)}, f32[4,8,128]{2,1,0:T(8,128)S(1)}) fusion(pred[4,128]{1,0:T(4,128)(4,1)S(1)} %broadcast_compare_fusion.4, pred[4,8192,128]{2,1,0:T(32,128)(4,1)S(1)} %bitcast_compare_fusion.2, bf16[16,4,8,8192]{3,2,1,0:T(8,128)(2,1)} %get-tuple-element.121, s32[]{:T(128)} %get-tuple-element.110), kind=kOutput, calls=%fused_computation.7.clone.1 | convolution fusion | flops 67116544 | bytes 4738048 | tf_op jit(solution)/shard_map/while/body/eval_jaxpr/pgk,pkt->pgt/dot_general | solution.py:76
  99.7 2.7 bitcast_compare_fusion.2
  102.4 3.1 %select_reduce_fusion.6 = (f32[4,128]{1,0:T(4,128)S(1)}, f32[4,8,128]{2,1,0:T(8,128)S(1)}) fusion(pred[4,128]{1,0:T(4,128)(4,1)S(1)} %broadcast_compare_fusion.4, pred[4,8192,128]{2,1,0:T(32,128)(4,1)S(1)} %bitcast_compare_fusion.2, bf16[16,4,8,8192]{3,2,1,0:T(8,128)(2,1)} %get-tuple-element.121, s32[]{:T(128)} %get-tuple-element.110), kind=kOutput, calls=%fused_computation.7.clone.1 | convolution fusion | flops 67116544 | bytes 4738048 | tf_op jit(solution)/shard_map/while/body/eval_jaxpr/pgk,pkt->pgt/dot_general | solution.py:76
  107.2 2.7 bitcast_compare_fusion.2
  109.9 3.1 %select_reduce_fusion.6 = (f32[4,128]{1,0:T(4,128)S(1)}, f32[4,8,128]{2,1,0:T(8,128)S(1)}) fusion(pred[4,128]{1,0:T(4,128)(4,1)S(1)} %broadcast_compare_fusion.4, pred[4,8192,128]{2,1,0:T(32,128)(4,1)S(1)} %bitcast_compare_fusion.2, bf16[16,4,8,8192]{3,2,1,0:T(8,128)(2,1)} %get-tuple-element.121, s32[]{:T(128)} %get-tuple-element.110), kind=kOutput, calls=%fused_computation.7.clone.1 | convolution fusion | flops 67116544 | bytes 4738048 | tf_op jit(solution)/shard_map/while/body/eval_jaxpr/pgk,pkt->pgt/dot_general | solution.py:76
  114.8 2.7 bitcast_compare_fusion.2
  117.4 3.1 %select_reduce_fusion.6 = (f32[4,128]{1,0:T(4,128)S(1)}, f32[4,8,128]{2,1,0:T(8,128)S(1)}) fusion(pred[4,128]{1,0:T(4,128)(4,1)S(1)} %broadcast_compare_fusion.4, pred[4,8192,128]{2,1,0:T(32,128)(4,1)S(1)} %bitcast_compare_fusion.2, bf16[16,4,8,8192]{3,2,1,0:T(8,128)(2,1)} %get-tuple-element.121, s32[]{:T(128)} %get-tuple-element.110), kind=kOutput, calls=%fused_computation.7.clone.1 | convolution fusion | flops 67116544 | bytes 4738048 | tf_op jit(solution)/shard_map/while/body/eval_jaxpr/pgk,pkt->pgt/dot_general | solution.py:76
  122.3 2.7 bitcast_compare_fusion.2
  124.9 3.1 %select_reduce_fusion.6 = (f32[4,128]{1,0:T(4,128)S(1)}, f32[4,8,128]{2,1,0:T(8,128)S(1)}) fusion(pred[4,128]{1,0:T(4,128)(4,1)S(1)} %broadcast_compare_fusion.4, pred[4,8192,128]{2,1,0:T(32,128)(4,1)S(1)} %bitcast_compare_fusion.2, bf16[16,4,8,8192]{3,2,1,0:T(8,128)(2,1)} %get-tuple-element.121, s32[]{:T(128)} %get-tuple-element.110), kind=kOutput, calls=%fused_computation.7.clone.1 | convolution fusion | flops 67116544 | bytes 4738048 | tf_op jit(solution)/shard_map/while/body/eval_jaxpr/pgk,pkt->pgt/dot_general | solution.py:76
  129.8 2.7 bitcast_compare_fusion.2
  132.5 3.1 %select_reduce_fusion.6 = (f32[4,128]{1,0:T(4,128)S(1)}, f32[4,8,128]{2,1,0:T(8,128)S(1)}) fusion(pred[4,128]{1,0:T(4,128)(4,1)S(1)} %broadcast_compare_fusion.4, pred[4,8192,128]{2,1,0:T(32,128)(4,1)S(1)} %bitcast_compare_fusion.2, bf16[16,4,8,8192]{3,2,1,0:T(8,128)(2,1)} %get-tuple-element.121, s32[]{:T(128)} %get-tuple-element.110), kind=kOutput, calls=%fused_computation.7.clone.1 | convolution fusion | flops 67116544 | bytes 4738048 | tf_op jit(solution)/shard_map/while/body/eval_jaxpr/pgk,pkt->pgt/dot_general | solution.py:76
  137.3 2.7 bitcast_compare_fusion.2
  140.0 3.1 %select_reduce_fusion.6 = (f32[4,128]{1,0:T(4,128)S(1)}, f32[4,8,128]{2,1,0:T(8,128)S(1)}) fusion(pred[4,128]{1,0:T(4,128)(4,1)S(1)} %broadcast_compare_fusion.4, pred[4,8192,128]{2,1,0:T(32,128)(4,1)S(1)} %bitcast_compare_fusion.2, bf16[16,4,8,8192]{3,2,1,0:T(8,128)(2,1)} %get-tuple-element.121, s32[]{:T(128)} %get-tuple-element.110), kind=kOutput, calls=%fused_computation.7.clone.1 | convolution fusion | flops 67116544 | bytes 4738048 | tf_op jit(solution)/shard_map/while/body/eval_jaxpr/pgk,pkt->pgt/dot_general | solution.py:76
  144.8 2.7 bitcast_compare_fusion.2
  147.5 3.1 %select_reduce_fusion.6 = (f32[4,128]{1,0:T(4,128)S(1)}, f32[4,8,128]{2,1,0:T(8,128)S(1)}) fusion(pred[4,128]{1,0:T(4,128)(4,1)S(1)} %broadcast_compare_fusion.4, pred[4,8192,128]{2,1,0:T(32,128)(4,1)S(1)} %bitcast_compare_fusion.2, bf16[16,4,8,8192]{3,2,1,0:T(8,128)(2,1)} %get-tuple-element.121, s32[]{:T(128)} %get-tuple-element.110), kind=kOutput, calls=%fused_computation.7.clone.1 | convolution fusion | flops 67116544 | bytes 4738048 | tf_op jit(solution)/shard_map/while/body/eval_jaxpr/pgk,pkt->pgt/dot_general | solution.py:76
  152.3 2.7 bitcast_compare_fusion.2
  155.0 3.1 %select_reduce_fusion.6 = (f32[4,128]{1,0:T(4,128)S(1)}, f32[4,8,128]{2,1,0:T(8,128)S(1)}) fusion(pred[4,128]{1,0:T(4,128)(4,1)S(1)} %broadcast_compare_fusion.4, pred[4,8192,128]{2,1,0:T(32,128)(4,1)S(1)} %bitcast_compare_fusion.2, bf16[16,4,8,8192]{3,2,1,0:T(8,128)(2,1)} %get-tuple-element.121, s32[]{:T(128)} %get-tuple-element.110), kind=kOutput, calls=%fused_computation.7.clone.1 | convolution fusion | flops 67116544 | bytes 4738048 | tf_op jit(solution)/shard_map/while/body/eval_jaxpr/pgk,pkt->pgt/dot_general | solution.py:76
  159.9 2.7 bitcast_compare_fusion.2
  162.5 3.1 %select_reduce_fusion.6 = (f32[4,128]{1,0:T(4,128)S(1)}, f32[4,8,128]{2,1,0:T(8,128)S(1)}) fusion(pred[4,128]{1,0:T(4,128)(4,1)S(1)} %broadcast_compare_fusion.4, pred[4,8192,128]{2,1,0:T(32,128)(4,1)S(1)} %bitcast_compare_fusion.2, bf16[16,4,8,8192]{3,2,1,0:T(8,128)(2,1)} %get-tuple-element.121, s32[]{:T(128)} %get-tuple-element.110), kind=kOutput, calls=%fused_computation.7.clone.1 | convolution fusion | flops 67116544 | bytes 4738048 | tf_op jit(solution)/shard_map/while/body/eval_jaxpr/pgk,pkt->pgt/dot_general | solution.py:76
  167.4 2.7 bitcast_compare_fusion.2
  170.0 3.1 %select_reduce_fusion.6 = (f32[4,128]{1,0:T(4,128)S(1)}, f32[4,8,128]{2,1,0:T(8,128)S(1)}) fusion(pred[4,128]{1,0:T(4,128)(4,1)S(1)} %broadcast_compare_fusion.4, pred[4,8192,128]{2,1,0:T(32,128)(4,1)S(1)} %bitcast_compare_fusion.2, bf16[16,4,8,8192]{3,2,1,0:T(8,128)(2,1)} %get-tuple-element.121, s32[]{:T(128)} %get-tuple-element.110), kind=kOutput, calls=%fused_computation.7.clone.1 | convolution fusion | flops 67116544 | bytes 4738048 | tf_op jit(solution)/shard_map/while/body/eval_jaxpr/pgk,pkt->pgt/dot_general | solution.py:76
  174.9 2.7 bitcast_compare_fusion.2
  177.6 3.1 %select_reduce_fusion.6 = (f32[4,128]{1,0:T(4,128)S(1)}, f32[4,8,128]{2,1,0:T(8,128)S(1)}) fusion(pred[4,128]{1,0:T(4,128)(4,1)S(1)} %broadcast_compare_fusion.4, pred[4,8192,128]{2,1,0:T(32,128)(4,1)S(1)} %bitcast_compare_fusion.2, bf16[16,4,8,8192]{3,2,1,0:T(8,128)(2,1)} %get-tuple-element.121, s32[]{:T(128)} %get-tuple-element.110), kind=kOutput, calls=%fused_computation.7.clone.1 | convolution fusion | flops 67116544 | bytes 4738048 | tf_op jit(solution)/shard_map/while/body/eval_jaxpr/pgk,pkt->pgt/dot_general | solution.py:76
  182.4 2.7 bitcast_compare_fusion.2
  185.1 3.1 %select_reduce_fusion.6 = (f32[4,128]{1,0:T(4,128)S(1)}, f32[4,8,128]{2,1,0:T(8,128)S(1)}) fusion(pred[4,128]{1,0:T(4,128)(4,1)S(1)} %broadcast_compare_fusion.4, pred[4,8192,128]{2,1,0:T(32,128)(4,1)S(1)} %bitcast_compare_fusion.2, bf16[16,4,8,8192]{3,2,1,0:T(8,128)(2,1)} %get-tuple-element.121, s32[]{:T(128)} %get-tuple-element.110), kind=kOutput, calls=%fused_computation.7.clone.1 | convolution fusion | flops 67116544 | bytes 4738048 | tf_op jit(solution)/shard_map/while/body/eval_jaxpr/pgk,pkt->pgt/dot_general | solution.py:76
  189.9 2.7 bitcast_compare_fusion.2
  192.6 3.1 %select_reduce_fusion.6 = (f32[4,128]{1,0:T(4,128)S(1)}, f32[4,8,128]{2,1,0:T(8,128)S(1)}) fusion(pred[4,128]{1,0:T(4,128)(4,1)S(1)} %broadcast_compare_fusion.4, pred[4,8192,128]{2,1,0:T(32,128)(4,1)S(1)} %bitcast_compare_fusion.2, bf16[16,4,8,8192]{3,2,1,0:T(8,128)(2,1)} %get-tuple-element.121, s32[]{:T(128)} %get-tuple-element.110), kind=kOutput, calls=%fused_computation.7.clone.1 | convolution fusion | flops 67116544 | bytes 4738048 | tf_op jit(solution)/shard_map/while/body/eval_jaxpr/pgk,pkt->pgt/dot_general | solution.py:76
  197.4 2.7 bitcast_compare_fusion.2
  200.1 3.1 %select_reduce_fusion.6 = (f32[4,128]{1,0:T(4,128)S(1)}, f32[4,8,128]{2,1,0:T(8,128)S(1)}) fusion(pred[4,128]{1,0:T(4,128)(4,1)S(1)} %broadcast_compare_fusion.4, pred[4,8192,128]{2,1,0:T(32,128)(4,1)S(1)} %bitcast_compare_fusion.2, bf16[16,4,8,8192]{3,2,1,0:T(8,128)(2,1)} %get-tuple-element.121, s32[]{:T(128)} %get-tuple-element.110), kind=kOutput, calls=%fused_computation.7.clone.1 | convolution fusion | flops 67116544 | bytes 4738048 | tf_op jit(solution)/shard_map/while/body/eval_jaxpr/pgk,pkt->pgt/dot_general | solution.py:76
  206.9 2.8 %copy.66 = bf16[4,64,2048]{2,1,0:T(8,128)(2,1)} copy(bf16[4,64,2048]{2,0,1:T(4,128)(2,1)} %all-to-all-done.1) | data formatting | bytes 2097152 | tf_op jit(solution)/shard_map/all_to_all | solution.py:104
  211.2 1.6 copy.67
  215.7 45.2 %all-gather = bf16[64,1,1024]{2,1,0:T(2,128)(2,1)S(1)} all-gather(bf16[1,1,1024]{2,1,0:T(2,128)(2,1)S(1)} %convert_element_type.94), channel_id=1, replica_groups=mesh['seq'=64,'head'=4] {'seq'}, dimensions={0}, use_global_device_ids=true | all-gather | bytes 133120 | tf_op jit(solution)/shard_map/all_gather | solution.py:115
  261.2 13.2 %all-reduce = bf16[32,128]{1,0:T(8,128)(2,1)S(1)} all-reduce(f32[32,128]{1,0:T(8,128)S(1)} %reduce_sum.75), channel_id=2, replica_groups=mesh['seq'=64,'head'=4] {'head'}, use_global_device_ids=true, to_apply=%region_15.16.clone | all-reduce | flops 4096 | bytes 24576
  (326 shorter events, 40.0 us)
Async XLA Ops:
  0.6 260.3 %copy-start = (bf16[2048,128]{1,0:T(8,128)(2,1)S(1)}, bf16[2048,128]{1,0:T(8,128)(2,1)}, u32[]{:S(2)}) copy-start(bf16[2048,128]{1,0:T(8,128)(2,1)} %param.17) | copy-start | bytes 1572868
  4.7 22.6 %all-to-all-start = ((bf16[4,64,1]{0,2,1:T(2,128)(2,1)}), bf16[4,64,1]{0,2,1:T(2,128)(2,1)S(1)}, u32[]{:S(2)}, u32[]{:S(2)}) async-start(bf16[4,64,1]{0,2,1:T(2,128)(2,1)} %copy.64), calls=%async_computation | async-start | bytes 65536 | tf_op jit(solution)/shard_map/all_to_all | solution.py:106
  17.9 15.2 %copy-start.3 = (s32[32,8]{0,1:T(8,128)S(1)}, s32[32,8]{0,1:T(8,128)}, u32[]{:S(2)}) copy-start(s32[32,8]{0,1:T(8,128)} %param.16) | copy-start | bytes 3076
  22.5 15.0 %copy-start.1 = (f32[2,4,32,256]{3,2,1,0:T(8,128)S(1)}, f32[2,4,32,256]{3,2,1,0:T(8,128)}, u32[]{:S(2)}) copy-start(f32[2,4,32,256]{3,2,1,0:T(8,128)} %param.14) | copy-start | bytes 786436
  27.3 45.9 %all-to-all-start.1 = ((bf16[4,64,2048]{2,0,1:T(4,128)(2,1)}), bf16[4,64,2048]{2,0,1:T(4,128)(2,1)}, u32[]{:S(2)}, u32[]{:S(2)}) async-start(bf16[4,64,2048]{2,0,1:T(4,128)(2,1)} %fusion.5), calls=%async_computation.1 | async-start | bytes 2097152 | tf_op jit(solution)/shard_map/all_to_all | solution.py:104
  73.2 138.1 %all-to-all-start.2 = ((bf16[4,64,2048]{2,0,1:T(4,128)(2,1)}), bf16[4,64,2048]{2,0,1:T(4,128)(2,1)S(1)}, u32[]{:S(2)}, u32[]{:S(2)}) async-start(bf16[4,64,2048]{2,0,1:T(4,128)(2,1)} %fusion.6), calls=%async_computation.2 | async-start | bytes 2097152 | tf_op jit(solution)/shard_map/all_to_all | solution.py:105
  83.5 121.1 %copy-start.4 = (u32[256]{0:T(256)S(1)}, u32[256]{0:T(256)}, u32[]{:S(2)}) copy-start(u32[256]{0:T(256)} %constant.73) | copy-start | bytes 3076
  215.7 59.2 %copy-start.2 = (bf16[1,1,1024]{2,1,0:T(2,128)(2,1)}, bf16[1,1,1024]{2,1,0:T(2,128)(2,1)S(1)}, u32[]{:S(2)}) copy-start(bf16[1,1,1024]{2,1,0:T(2,128)(2,1)S(1)} %convert_element_type.94) | copy-start | bytes 6148
where the time goes:
time: 279 us; the launch traced here: 275 us
  local copies, waits for them, and re-layouts  66.1 us (24%)
  matrix products  64.2 us (23%)
  blocking collectives  58.4 us (21%)
  other arithmetic  49.9 us (18%)
  starting transfers between devices  29.2 us (10%)
  waiting for transfers between devices  4.83 us (2%)
    dot_general x16, matrix products, score_group(): jnp.einsum('pgk,pkt->pgt', tab, onehot, preferred_element_type=jnp.float32)  50.1 us
    all_gather x1, blocking collectives, shards(): piece = lax.all_gather(flat, 'seq', axis=0, tiled=True)  45.2 us
    eq x16, other arithmetic, score_group(): code[:, :, None, :] == lax.iota(jnp.int32, cent)[None, None, :, None]  42.6 us
    eq x16, local copies, waits for them, and re-layouts, score_group(): code[:, :, None, :] == lax.iota(jnp.int32, cent)[None, None, :, None]  13.6 us
    another operation x1, local copies, waits for them, and re-layouts, shards(): table.reshape(steps_count, step_rows, group, nsub * cent)  13.5 us
    unnamed x1, blocking collectives  13.2 us
    all_to_all x1, starting transfers between devices, shards(): lax.all_to_all(send_lens, 'seq', split_axis=1, concat_axis=1, tiled=True)  13.1 us
    convert_element_type x1, local copies, waits for them, and re-layouts, shards(): table = table.astype(jnp.bfloat16).reshape(pairs, group, nsub * cent)  11.4 us
  transfers between devices with their start and end apart: 3, of which 1 were waited for; matrix products, arithmetic and copies ran while one was open for 62% of the time, Pallas kernels for 0%

commit v1 on v0

v1 whole, which is shorter than its diff:
```python
import functools

import jax
import jax.numpy as jnp
from jax import lax
from jax.experimental import pallas as pl
from jax.experimental.pallas import tpu as pltpu
from jax.sharding import PartitionSpec as P

MESH = pl.DeviceIdType.MESH
NEG = -1e30
LIVE = -5e29
F32 = jnp.float32
BF16 = jnp.bfloat16
SCALE = 128 ** -0.5


def iota(shape, axis):
    return lax.broadcasted_iota(jnp.int32, shape, axis)


def lane_reduce(x, lane, op):
    for s in (1, 2, 4, 8):
        up = pltpu.roll(x, s, 1)
        down = pltpu.roll(x, 128 - s, 1)
        x = op(x, jnp.where((lane & s) != 0, up, down))
    return x


def kernel(
    q_hbm, k_hbm, v_hbm, codes_hbm, cent_hbm, picks_hbm, len_hbm, w_hbm,
    est_ref, att_ref, lay_ref,
    q, k, v, codes, cent, picks, lens, w,
    bias, valid, q2, acc, send1, recv1, send2, recv2, gath, g32, part, recv5,
    in_sem, k_sem, v_sem, s1, r1, s2, r2, s3, r3, s4, r4, s5, r5,
):
    seq = lax.axis_index("seq")
    x = lax.axis_index("head")
    z = seq // 8
    i = lax.rem(seq, 8)

    def local(src, dst, n):
        return pltpu.make_async_copy(src, dst, in_sem.at[n])

    loads = [
        local(picks_hbm, picks, 0), local(len_hbm, lens, 1), local(q_hbm, q, 2),
        local(codes_hbm, codes, 3), local(cent_hbm, cent, 4), local(w_hbm, w, 5),
    ]
    for c in loads[:3]:
        c.start()

    def order(t):
        return 4 + ((t + 1) // 2) * (1 - 2 * lax.rem(t, 2))

    def kv_copies(t):
        j = lax.rem(i + order(t), 8)
        y_, h_ = j // 2, lax.rem(j, 2)
        return (
            pltpu.make_async_copy(k_hbm.at[:, y_, h_], k.at[t], k_sem.at[t]),
            pltpu.make_async_copy(v_hbm.at[:, y_, h_], v.at[t], v_sem.at[t]),
        )

    def kv_start(t, carry):
        for c in kv_copies(t):
            c.start()
        return carry

    lax.fori_loop(0, 8, kv_start, 0)
    for c in loads[3:]:
        c.start()

    barrier = pltpu.get_barrier_semaphore()
    for n in range(1, 8):
        pl.semaphore_signal(barrier, inc=1, device_id=(z * 8 + lax.rem(i + n, 8), x), device_id_type=MESH)
        pl.semaphore_signal(barrier, inc=1, device_id=(lax.rem(z + n, 8) * 8 + i, x), device_id_type=MESH)
    for n in range(1, 4):
        pl.semaphore_signal(barrier, inc=1, device_id=(seq, lax.rem(x + n, 4)), device_id_type=MESH)

    lane = iota((8, 128), 1)
    block_of = iota((32, 128), 1) // 16

    loads[0].wait()
    loads[1].wait()
    spread = jnp.where(iota((8, 128), 1) // 16 == iota((8, 128), 0), 1.0, 0.0)
    len_rows = lens[...].astype(F32).T
    len_lane = jnp.dot(len_rows, spread, preferred_element_type=F32)
    place = (iota((32, 128), 1) & 15).astype(F32)
    is_valid = place < len_lane
    valid[...] = jnp.where(is_valid, 0.0, NEG)
    for h in range(2):
        near = picks[pl.ds(h, 32, stride=2), :] - seq * 8
        chosen = jnp.zeros((32, 128), F32)
        for j in range(8):
            hit = jnp.max(jnp.where(near == j, 1.0, 0.0), axis=1, keepdims=True)
            chosen = jnp.where(block_of == j, hit, chosen)
        bias[h] = jnp.where(is_valid & (chosen > 0.5), 0.0, NEG)

    loads[2].wait()

    def bundle(t, j):
        y_, h_ = j // 2, lax.rem(j, 2)
        for c in kv_copies(t):
            c.wait()
        off = bias[h_, pl.ds(y_, 8, stride=4), :]
        stat = jnp.zeros((8, 128), F32)
        for n in range(8):
            s = lax.dot_general(
                q[n * 4 + y_, h_], k[t, n], (((1,), (1,)), ((), ())), preferred_element_type=F32
            ) * SCALE + off[n : n + 1]
            top = jnp.max(s, axis=1, keepdims=True).astype(BF16).astype(F32)
            weight = jnp.where(s > LIVE, jnp.exp(s - top), 0.0)
            total = jnp.sum(weight, axis=1, keepdims=True)
            total_hi = total.astype(BF16).astype(F32)
            part_sum = jnp.dot(weight.astype(BF16), v[t, n], preferred_element_type=F32)
            send1[j, n] = part_sum.astype(BF16)
            stat = jnp.where(lane == n, top, stat)
            stat = jnp.where(lane == 16 + n, total_hi, stat)
            stat = jnp.where(lane == 32 + n, total - total_hi, stat)
        send1[j, 8] = stat.astype(BF16)

    def copy1(n):
        j = lax.rem(i + n, 8)
        return pltpu.make_async_remote_copy(
            send1.at[j], recv1.at[n], s1.at[n], r1.at[n], device_id=(z * 8 + j, x), device_id_type=MESH
        )

    pl.semaphore_wait(barrier, 17)

    def send_bundle(t, carry):
        n = order(t)
        bundle(t, lax.rem(i + n, 8))
        copy1(n).start()
        return carry

    lax.fori_loop(0, 7, send_bundle, 0)
    bundle(7, i)

    loads[3].wait()
    loads[4].wait()
    for h in range(2):
        q2[h] = q[:, h].reshape(256, 128)

    def table_step(h, m):
        row = iota((16, 256), 0) & 3
        pattern = jnp.broadcast_to(cent[h, 3, pl.ds(m, 1), :], (16, 256))
        for s in range(3):
            pattern = jnp.where(row == s, cent[h, s, pl.ds(m, 1), :], pattern)
        pattern = pattern * SCALE
        hi = pattern.astype(BF16)
        lo = (pattern - hi.astype(F32)).astype(BF16)
        own = jnp.where(iota((16, 128), 1) // 4 == m, 1.0, 0.0).astype(BF16)
        lhs = q2[h] * jnp.concatenate([own] * 16, axis=0)
        rhs = jnp.concatenate([hi] * 8 + [lo] * 8, axis=0)
        table = jnp.dot(jnp.concatenate([lhs, lhs], axis=1), rhs, preferred_element_type=F32)
        for b in range(32):
            code = jnp.broadcast_to(codes[b, h, pl.ds(m, 1), :], (8, 128))
            index = code & 127
            rows = table[b * 8 : b * 8 + 8]
            first = jnp.take_along_axis(rows[:, :128], index, axis=1, mode="promise_in_bounds")
            second = jnp.take_along_axis(rows[:, 128:], index, axis=1, mode="promise_in_bounds")
            acc[pl.ds((h * 32 + b) * 8, 8), :] += jnp.where(code > 127, second, first)

    def estimate(h, low, high):
        def step(m, carry):
            table_step(h, m)
            return carry

        lax.fori_loop(low, high, step, 0)

    def finish_estimates(h):
        rows = []
        for bb in range(4):
            base = (h * 32 + bb * 8) * 8
            off = valid[bb * 8 : bb * 8 + 8, :]
            parts = [acc[pl.ds(base + g, 8, stride=8), :] + off for g in range(8)]
            top = functools.reduce(jnp.maximum, parts)
            top = lane_reduce(top, lane, jnp.maximum)
            mass = functools.reduce(jnp.add, [jnp.where(off == 0.0, jnp.exp(a - top), 0.0) for a in parts])
            mass = lane_reduce(mass, lane, jnp.add)
            rows.append(top + jnp.log(mass))
        rows = jnp.concatenate(rows, axis=0)
        pick = jnp.where(iota((8, 128), 1) == iota((8, 128), 0) * 16, 1.0, 0.0)
        est_ref[h] = lax.dot_general(
            pick, rows, (((1,), (1,)), ((), ())), precision=lax.Precision.HIGHEST, preferred_element_type=F32
        )

    def zero(n, carry):
        acc[pl.ds(pl.multiple_of(n * 32, 32), 32), :] = jnp.zeros((32, 128), F32)
        return carry

    lax.fori_loop(0, 16, zero, 0)
    estimate(0, 0, 20)

    def merge(stats):
        top = functools.reduce(jnp.maximum, stats)
        scales = [jnp.exp(a - top) for a in stats]
        totals = [
            (pltpu.roll(a, 112, 1) + pltpu.roll(a, 96, 1)) * e for a, e in zip(stats, scales)
        ]
        return top, scales, functools.reduce(jnp.add, totals)

    for n in range(1, 8):
        copy1(n).wait_recv()
    sources = [send1.at[i]] + [recv1.at[n] for n in range(1, 8)]
    top, scales, total = merge([a[8].astype(F32) for a in sources])
    total_hi = total.astype(BF16).astype(F32)
    stat = jnp.where(lane < 8, top, jnp.where(
        lane < 32, pltpu.roll(total_hi, 16, 1), pltpu.roll(total - total_hi, 32, 1)))
    stat = stat.astype(BF16)
    for n in range(8):
        summed = functools.reduce(
            jnp.add, [e[:, n : n + 1] * a[n].astype(F32) for a, e in zip(sources, scales)]
        )
        send2[n, 0] = summed.astype(BF16)
        send2[n, 1] = stat

    def copy2(n):
        to = lax.rem(z + n, 8)
        return pltpu.make_async_remote_copy(
            send2.at[to], recv2.at[n], s2.at[n], r2.at[n], device_id=(to * 8 + i, x), device_id_type=MESH
        )

    for n in (4, 3, 5, 2, 6, 1, 7):
        copy2(n).start()
    estimate(0, 20, 32)
    estimate(1, 0, 8)

    for n in range(1, 8):
        copy2(n).wait_recv()
    sources = [send2.at[z]] + [recv2.at[n] for n in range(1, 8)]
    top, scales, total = merge([a[1].astype(F32) for a in sources])
    back = lax.rem(128 - z, 128)
    summed = functools.reduce(
        jnp.add, [pltpu.roll(e, back, 1)[:, 0:1] * a[0].astype(F32) for a, e in zip(sources, scales)]
    )
    head_out = (summed / pltpu.roll(total, back, 1)[:, 0:1]).astype(BF16)
    gath[i, z] = head_out
    att_ref[...] = head_out

    def copy3(n):
        to = lax.rem(z + n, 8)
        return pltpu.make_async_remote_copy(
            gath.at[i, z], gath.at[i, z], s3.at[n], r3.at[n], device_id=(to * 8 + i, x), device_id_type=MESH
        )

    def arrived3(n):
        slot = gath.at[i, lax.rem(z + 8 - n, 8)]
        return pltpu.make_async_remote_copy(
            slot, slot, s3.at[n], r3.at[n], device_id=(seq, x), device_id_type=MESH
        )

    for n in (4, 3, 5, 2, 6, 1, 7):
        copy3(n).start()
    estimate(1, 8, 24)
    for n in range(1, 8):
        arrived3(n).wait_recv()

    def copy4(n):
        to = lax.rem(i + n, 8)
        return pltpu.make_async_remote_copy(
            gath.at[i], gath.at[i], s4.at[n], r4.at[n], device_id=(z * 8 + to, x), device_id_type=MESH
        )

    def arrived4(n):
        slot = gath.at[lax.rem(i + 8 - n, 8)]
        return pltpu.make_async_remote_copy(
            slot, slot, s4.at[n], r4.at[n], device_id=(seq, x), device_id_type=MESH
        )

    for n in (4, 3, 5, 2, 6, 1, 7):
        copy4(n).start()
    estimate(1, 24, 32)
    finish_estimates(0)
    loads[5].wait()
    for n in range(1, 8):
        arrived4(n).wait_recv()

    for n in range(8):
        g32[pl.ds(n * 64, 64), :] = gath[n].astype(F32).reshape(64, 128)
    products = []
    for h in range(2):
        columns = []
        for g in range(8):
            columns.append(jnp.concatenate(
                [g32[pl.ds((2 * y_ + h) * 64 + g, 8, stride=8), :] for y_ in range(4)], axis=0
            ).astype(BF16))
        products.append(jnp.dot(
            jnp.concatenate(columns, axis=1), w[pl.ds(h * 1024, 1024), :], preferred_element_type=F32
        ))
    product = products[0] + products[1]
    for y_ in range(4):
        part[pl.ds(y_, 8, stride=4), :] = product[y_ * 8 : y_ * 8 + 8]

    def copy5(n):
        to = lax.rem(x + n, 4)
        return pltpu.make_async_remote_copy(
            part.at[pl.ds(pl.multiple_of(to * 8, 8), 8), :], recv5.at[n], s5.at[n], r5.at[n],
            device_id=(seq, to), device_id_type=MESH,
        )

    for n in (2, 1, 3):
        copy5(n).start()
    finish_estimates(1)
    result = part[pl.ds(pl.multiple_of(x * 8, 8), 8), :]
    for n in range(1, 4):
        copy5(n).wait_recv()
        result = result + recv5[n]
    lay_ref[...] = result.astype(BF16)

    for n in range(1, 8):
        copy1(n).wait_send()
        copy2(n).wait_send()
        copy3(n).wait_send()
        copy4(n).wait_send()
    for n in range(1, 4):
        copy5(n).wait_send()


def shards(queries, keys, values, codes, centroids, picks, block_len, out_weight):
    vmem = pltpu.VMEM
    dma = pltpu.SemaphoreType.DMA
    est, att, lay = pl.pallas_call(
        kernel,
        out_shape=(
            jax.ShapeDtypeStruct((2, 8, 32), F32),
            jax.ShapeDtypeStruct((8, 128), BF16),
            jax.ShapeDtypeStruct((8, 128), BF16),
        ),
        in_specs=[pl.BlockSpec(memory_space=pl.ANY)] * 8,
        out_specs=[pl.BlockSpec(memory_space=vmem)] * 3,
        scratch_shapes=[
            vmem((32, 2, 8, 128), BF16),
            vmem((8, 8, 128, 128), BF16),
            vmem((8, 8, 128, 128), BF16),
            vmem((32, 2, 32, 128), jnp.int32),
            vmem((2, 4, 32, 256), F32),
            vmem((64, 64), jnp.int32),
            vmem((8, 32), jnp.int32),
            vmem((2048, 128), BF16),
            vmem((2, 32, 128), F32),
            vmem((32, 128), F32),
            vmem((2, 256, 128), BF16),
            vmem((512, 128), F32),
            vmem((8, 9, 8, 128), BF16),
            vmem((8, 9, 8, 128), BF16),
            vmem((8, 2, 8, 128), BF16),
            vmem((8, 2, 8, 128), BF16),
            vmem((8, 8, 8, 128), BF16),
            vmem((512, 128), F32),
            vmem((32, 128), F32),
            vmem((4, 8, 128), F32),
            dma((6,)), dma((8,)), dma((8,)),
            dma((8,)), dma((8,)), dma((8,)), dma((8,)), dma((8,)), dma((8,)),
            dma((8,)), dma((8,)), dma((4,)), dma((4,)),
        ],
        compiler_params=pltpu.CompilerParams(
            collective_id=0, has_side_effects=True, vmem_limit_bytes=48 << 20
        ),
        name="decode",
    )(
        queries.reshape(32, 2, 8, 128),
        keys.reshape(8, 4, 2, 128, 128),
        values.reshape(8, 4, 2, 128, 128),
        codes,
        centroids,
        picks.reshape(64, 64),
        block_len.T,
        out_weight,
    )
    return est.transpose(2, 0, 1), att.reshape(1, 1, 1024), lay


def solution(mesh):
    placed = (
        P(None, "head", None),
        P(None, "head", "seq", None),
        P(None, "head", "seq", None),
        P(None, "head", None, "seq"),
        P("head", None, None, None),
        P(None, "head", None),
        P(None, "seq"),
        P("head", "seq"),
    )
    return jax.shard_map(
        shards,
        mesh=mesh,
        in_specs=placed,
        out_specs=(P(None, "head", "seq"), P("seq", "head", None), P("head", "seq")),
        check_vma=False,
    )
```

time: 279 us -> 68.6 us (0.25); the launches traced: 275 us -> 68.2 us
  matrix products: 64.2 us -> 0 us
  blocking collectives: 58.4 us -> 0 us
  Pallas kernels: 0 us -> 57 us
  local copies, waits for them, and re-layouts: 66.1 us -> 10.5 us
  other arithmetic: 49.9 us -> 0 us
  starting transfers between devices: 29.2 us -> 0 us
  waiting for transfers between devices: 4.83 us -> 0 us
    dot_general x23 -> x0, matrix products: 64.2 us -> none  [the longest x16 50.1 us: score_group(): jnp.einsum('pgk,pkt->pgt', tab, onehot, preferred_element_type=jnp.float32)]
    pallas_call x0 -> x1, Pallas kernels: none -> 57 us  [shards(): pl.pallas_call(kernel, out_shape=(jax.ShapeDtypeStruct((2, 8, 32), F32),...]
    all_gather x1 -> x0, blocking collectives: 45.2 us -> none  [shards(): piece = lax.all_gather(flat, 'seq', axis=0, tiled=True)]
    eq x16 -> x0, other arithmetic: 42.6 us -> none  [score_group(): code[:, :, None, :] == lax.iota(jnp.int32, cent)[None, None, :, None]]
    all_to_all x3 -> x0, starting transfers between devices: 29.2 us -> none  [the longest x1 13.1 us: shards(): lax.all_to_all(send_lens, 'seq', split_axis=1, concat_axis=1, tiled=True)]
    eq x16 -> x0, local copies, waits for them, and re-layouts: 13.6 us -> none  [score_group(): code[:, :, None, :] == lax.iota(jnp.int32, cent)[None, None, :, None]]
    another operation x1 -> x0, local copies, waits for them, and re-layouts: 13.5 us -> none  [shards(): table.reshape(steps_count, step_rows, group, nsub * cent)]
    unnamed x1 -> x0, blocking collectives: 13.2 us -> none
  transfers between devices with their start and end apart: 3 -> 0, of which waited for: 1 -> 0; matrix products, arithmetic and copies ran while one was open for 62% -> 0% of each run, Pallas kernels for 0% -> 0%
where the time goes in v1:
time: 68.6 us; the launch traced here: 68.2 us
  Pallas kernels  57 us (83%)
  local copies, waits for them, and re-layouts  10.5 us (15%)
    pallas_call x1, Pallas kernels, shards(): pl.pallas_call(kernel, out_shape=(jax.ShapeDtypeStruct((2, 8, 32), F32),...  57 us
    unnamed x18, local copies, waits for them, and re-layouts  9.91 us

profile of v1, /device:TPU:1, one launch (start us, length us, event | category | flops | bytes accessed | tf_op | source)
XLA Modules:
  0.0 68.2 jit_solution(1743872306777631121)
XLA Ops:
  0.6 0.0 copy-start
  0.6 1.6 %copy-done = bf16[32,2,128,128]{3,2,1,0:T(8,128)(2,1)S(1)} copy-done((bf16[32,2,128,128]{3,2,1,0:T(8,128)(2,1)S(1)}, bf16[32,2,128,128]{3,2,1,0:T(8,128)(2,1)}, u32[]{:S(2)}) %copy-start) | copy-done | bytes 2097176
  2.2 0.0 copy-start.1
  2.2 1.6 %copy-done.1 = bf16[32,2,128,128]{3,2,1,0:T(8,128)(2,1)S(1)} copy-done((bf16[32,2,128,128]{3,2,1,0:T(8,128)(2,1)S(1)}, bf16[32,2,128,128]{3,2,1,0:T(8,128)(2,1)}, u32[]{:S(2)}) %copy-start.1) | copy-done | bytes 2097176
  3.8 0.0 copy-start.2
  3.8 1.2 %copy-done.2 = s32[32,2,32,128]{3,2,1,0:T(8,128)S(1)} copy-done((s32[32,2,32,128]{3,2,1,0:T(8,128)S(1)}, s32[32,2,32,128]{3,2,1,0:T(8,128)}, u32[]{:S(2)}) %copy-start.2) | copy-done | bytes 1048600
  5.0 0.0 copy-start.3
  5.0 1.0 %copy-done.3 = bf16[2048,128]{1,0:T(8,128)(2,1)S(1)} copy-done((bf16[2048,128]{1,0:T(8,128)(2,1)S(1)}, bf16[2048,128]{1,0:T(8,128)(2,1)}, u32[]{:S(2)}) %copy-start.3) | copy-done | bytes 524312
  6.1 0.0 copy-start.4
  6.1 0.9 %copy-done.4 = f32[2,4,32,256]{3,2,1,0:T(8,128)S(1)} copy-done((f32[2,4,32,256]{3,2,1,0:T(8,128)S(1)}, f32[2,4,32,256]{3,2,1,0:T(8,128)}, u32[]{:S(2)}) %copy-start.4) | copy-done | bytes 262168
  7.0 0.0 copy-start.5
  7.0 0.9 %copy-done.5 = bf16[32,16,128]{2,1,0:T(8,128)(2,1)S(1)} copy-done((bf16[32,16,128]{2,1,0:T(8,128)(2,1)S(1)}, bf16[32,16,128]{2,1,0:T(8,128)(2,1)}, u32[]{:S(2)}) %copy-start.5) | copy-done | bytes 131096
  7.9 0.0 copy-start.6
  7.9 0.8 %copy-done.6 = s32[32,2,64]{2,1,0:T(2,128)S(1)} copy-done((s32[32,2,64]{2,1,0:T(2,128)S(1)}, s32[32,2,64]{2,1,0:T(2,128)}, u32[]{:S(2)}) %copy-start.6) | copy-done | bytes 16408
  8.7 0.0 copy-start.7
  8.7 0.7 %copy-done.7 = s32[32,8]{0,1:T(8,128)S(1)} copy-done((s32[32,8]{0,1:T(8,128)S(1)}, s32[32,8]{0,1:T(8,128)}, u32[]{:S(2)}) %copy-start.7) | copy-done | bytes 1048
  9.4 57.0 %decode.1 = (f32[2,8,32]{2,1,0:T(8,128)S(1)}, bf16[8,128]{1,0:T(8,128)(2,1)S(1)}, bf16[8,128]{1,0:T(8,128)(2,1)S(1)}) custom-call(bf16[32,2,8,128]{3,2,1,0:T(8,128)(2,1)S(1)} %bitcast.8, bf16[8,4,2,128,128]{4,3,2,1,0:T(8,128)(2,1)S(1)} %bitcast.6, bf16[8,4,2,128,128]{4,3,2,1,0:T(8,128)(2,1)S(1)} %bitcast.7, s32[32,2,32,128]{3,2,1,0:T(8,128)S(1)} %copy-done.2, ...), custom_call_target="tpu_custom_call" | custom-call | tf_op jit(solution)/shard_map/decode/pallas_call | solution.py:322
  66.4 0.6 reshape.25
  67.0 0.6 copy.13
  67.6 0.6 copy.14
Async XLA Ops:
  0.6 1.6 %copy-start = (bf16[32,2,128,128]{3,2,1,0:T(8,128)(2,1)S(1)}, bf16[32,2,128,128]{3,2,1,0:T(8,128)(2,1)}, u32[]{:S(2)}) copy-start(bf16[32,2,128,128]{3,2,1,0:T(8,128)(2,1)} %param.9) | copy-start | bytes 6291460
  2.2 1.6 %copy-start.1 = (bf16[32,2,128,128]{3,2,1,0:T(8,128)(2,1)S(1)}, bf16[32,2,128,128]{3,2,1,0:T(8,128)(2,1)}, u32[]{:S(2)}) copy-start(bf16[32,2,128,128]{3,2,1,0:T(8,128)(2,1)} %param.10) | copy-start | bytes 6291460
  3.8 1.2 %copy-start.2 = (s32[32,2,32,128]{3,2,1,0:T(8,128)S(1)}, s32[32,2,32,128]{3,2,1,0:T(8,128)}, u32[]{:S(2)}) copy-start(s32[32,2,32,128]{3,2,1,0:T(8,128)} %codes_hbm.1) | copy-start | bytes 3145732
  5.0 1.0 %copy-start.3 = (bf16[2048,128]{1,0:T(8,128)(2,1)S(1)}, bf16[2048,128]{1,0:T(8,128)(2,1)}, u32[]{:S(2)}) copy-start(bf16[2048,128]{1,0:T(8,128)(2,1)} %w_hbm.1) | copy-start | bytes 1572868
  6.1 0.9 %copy-start.4 = (f32[2,4,32,256]{3,2,1,0:T(8,128)S(1)}, f32[2,4,32,256]{3,2,1,0:T(8,128)}, u32[]{:S(2)}) copy-start(f32[2,4,32,256]{3,2,1,0:T(8,128)} %cent_hbm.1) | copy-start | bytes 786436
  7.0 0.9 %copy-start.5 = (bf16[32,16,128]{2,1,0:T(8,128)(2,1)S(1)}, bf16[32,16,128]{2,1,0:T(8,128)(2,1)}, u32[]{:S(2)}) copy-start(bf16[32,16,128]{2,1,0:T(8,128)(2,1)} %param.8) | copy-start | bytes 393220
  7.9 0.8 %copy-start.6 = (s32[32,2,64]{2,1,0:T(2,128)S(1)}, s32[32,2,64]{2,1,0:T(2,128)}, u32[]{:S(2)}) copy-start(s32[32,2,64]{2,1,0:T(2,128)} %param.13) | copy-start | bytes 49156
  8.7 0.7 %copy-start.7 = (s32[32,8]{0,1:T(8,128)S(1)}, s32[32,8]{0,1:T(8,128)}, u32[]{:S(2)}) copy-start(s32[32,8]{0,1:T(8,128)} %param.14) | copy-start | bytes 3076

commit v2 on v1

v2 whole, which is shorter than its diff:
```python
import functools

import jax
import jax.numpy as jnp
from jax import lax
from jax.experimental import pallas as pl
from jax.experimental.pallas import tpu as pltpu
from jax.sharding import PartitionSpec as P

MESH = pl.DeviceIdType.MESH
NEG = -1e30
LIVE = -5e29
F32 = jnp.float32
BF16 = jnp.bfloat16
SCALE = 128 ** -0.5
GAP1 = 32
GAP2 = 32


def iota(shape, axis):
    return lax.broadcasted_iota(jnp.int32, shape, axis)


def lane_reduce(x, lane, op):
    for s in (1, 2, 4, 8):
        up = pltpu.roll(x, s, 1)
        down = pltpu.roll(x, 128 - s, 1)
        x = op(x, jnp.where((lane & s) != 0, up, down))
    return x


def lookup(rows, index):
    numbers = lax.GatherDimensionNumbers(
        offset_dims=(), collapsed_slice_dims=(1,), start_index_map=(1,),
        operand_batching_dims=(0,), start_indices_batching_dims=(0,),
    )
    return lax.gather(rows, index[..., None], numbers, (1, 1), mode=lax.GatherScatterMode.PROMISE_IN_BOUNDS)


def kernel(
    q_hbm, k_hbm, v_hbm, codes_hbm, cent_hbm, picks_hbm, len_hbm, w_hbm,
    est_ref, att_ref, lay_ref,
    q, k, v, codes, cent, picks, lens, w,
    bias, valid, q2, tab, acc, score, wide, send1, recv1, send2, recv2, gath, g32, part, recv5,
    in_sem, k_sem, v_sem, s1, r1, s2, r2, s4, r4, s5, r5,
):
    seq = lax.axis_index("seq")
    x = lax.axis_index("head")
    z = seq // 8
    i = lax.rem(seq, 8)

    def local(src, dst, n):
        return pltpu.make_async_copy(src, dst, in_sem.at[n])

    loads = [
        local(picks_hbm, picks, 0), local(len_hbm, lens, 1), local(q_hbm, q, 2),
        local(codes_hbm, codes, 3), local(cent_hbm, cent, 4), local(w_hbm, w, 5),
    ]
    kv = [
        (
            pltpu.make_async_copy(k_hbm.at[pl.ds(c * 8, 8)], k.at[pl.ds(c * 8, 8)], k_sem.at[c]),
            pltpu.make_async_copy(v_hbm.at[pl.ds(c * 8, 8)], v.at[pl.ds(c * 8, 8)], v_sem.at[c]),
        )
        for c in range(4)
    ]
    for c in loads[:3]:
        c.start()
    for c in kv:
        c[0].start()
    for c in kv:
        c[1].start()
    for c in loads[3:]:
        c.start()

    barrier = pltpu.get_barrier_semaphore()
    for n in range(1, 8):
        pl.semaphore_signal(barrier, inc=1, device_id=(z * 8 + lax.rem(i + n, 8), x), device_id_type=MESH)
        pl.semaphore_signal(barrier, inc=1, device_id=(lax.rem(z + n, 8) * 8 + i, x), device_id_type=MESH)
    for n in range(1, 4):
        pl.semaphore_signal(barrier, inc=1, device_id=(seq, lax.rem(x + n, 4)), device_id_type=MESH)

    lane = iota((8, 128), 1)
    block_of = iota((32, 128), 1) // 16

    loads[0].wait()
    loads[1].wait()
    spread = jnp.where(iota((8, 128), 1) // 16 == iota((8, 128), 0), 1.0, 0.0)
    len_rows = lens[...].astype(F32).T
    len_lane = jnp.dot(len_rows, spread, preferred_element_type=F32)
    place = (iota((32, 128), 1) & 15).astype(F32)
    is_valid = place < len_lane
    valid[...] = jnp.where(is_valid, 0.0, NEG)
    for h in range(2):
        near = picks[pl.ds(h, 32, stride=2), :] - seq * 8
        chosen = jnp.zeros((32, 128), F32)
        for j in range(8):
            hit = jnp.max(jnp.where(near == j, 1.0, 0.0), axis=1, keepdims=True)
            chosen = jnp.where(block_of == j, hit, chosen)
        bias[h] = jnp.where(is_valid & (chosen > 0.5), 0.0, NEG)

    loads[2].wait()
    for b in range(32):
        if b % 8 == 0:
            kv[b // 8][0].wait()
        both = lax.dot_general(
            q[b], k[b].reshape(256, 128), (((1,), (1,)), ((), ())), preferred_element_type=F32
        ) * SCALE
        score[b, 0] = both[:8, :128] + bias[0, b : b + 1, :]
        score[b, 1] = both[8:, 128:] + bias[1, b : b + 1, :]
    stats = [jnp.zeros((8, 128), F32)] * 8
    for c in range(4):
        tiles = [(b, h) for b in range(c * 8, c * 8 + 8) for h in range(2)]
        scores = [score[b, h] for b, h in tiles]
        tops = [jnp.max(s, axis=1, keepdims=True).astype(BF16).astype(F32) for s in scores]
        weights = [jnp.where(s > LIVE, jnp.exp(s - t), 0.0) for s, t in zip(scores, tops)]
        totals = [jnp.sum(e, axis=1, keepdims=True) for e in weights]
        for (b, h), top, weight, total in zip(tiles, tops, weights, totals):
            hi = weight.astype(BF16).astype(F32)
            wide[b, pl.ds(h * 8, 8), :] = hi
            wide[b, pl.ds(16 + h * 8, 8), :] = weight - hi
            j, n = (b % 4) * 2 + h, b // 4
            total_hi = total.astype(BF16).astype(F32)
            stat = jnp.where(lane == n, top, stats[j])
            stat = jnp.where(lane == 16 + n, total_hi, stat)
            stats[j] = jnp.where(lane == 32 + n, total - total_hi, stat)
    for j in range(8):
        send1[j, 8] = stats[j].astype(BF16)
    for b in range(32):
        if b % 8 == 0:
            kv[b // 8][1].wait()
        both = jnp.dot(
            wide[b].astype(BF16), jnp.concatenate([v[b, 0], v[b, 1]], axis=1), preferred_element_type=F32
        )
        for h in range(2):
            cols = slice(h * 128, h * 128 + 128)
            send1[(b % 4) * 2 + h, b // 4] = (
                both[h * 8 : h * 8 + 8, cols] + both[16 + h * 8 : 24 + h * 8, cols]
            ).astype(BF16)

    def copy1(n):
        j = lax.rem(i + n, 8)
        return pltpu.make_async_remote_copy(
            send1.at[j], recv1.at[n], s1.at[n], r1.at[n], device_id=(z * 8 + j, x), device_id_type=MESH
        )

    pl.semaphore_wait(barrier, 17)
    for n in (4, 3, 5, 2, 6, 1, 7):
        copy1(n).start()

    def table_one(h, m):
        row = iota((16, 256), 0) & 3
        pattern = jnp.broadcast_to(cent[h, 3, pl.ds(m, 1), :], (16, 256))
        for s in range(3):
            pattern = jnp.where(row == s, cent[h, s, pl.ds(m, 1), :], pattern)
        pattern = pattern * SCALE
        hi = pattern.astype(BF16)
        lo = (pattern - hi.astype(F32)).astype(BF16)
        own = jnp.where(iota((16, 128), 1) // 4 == m, 1.0, 0.0).astype(BF16)
        lhs = q2[h] * jnp.concatenate([own] * 16, axis=0)
        rhs = jnp.concatenate([hi] * 8 + [lo] * 8, axis=0)
        return jnp.dot(jnp.concatenate([lhs, lhs], axis=1), rhs, preferred_element_type=F32)

    def tables(low, high):
        def step(t, carry):
            h, m = t // 16, lax.rem(t, 16) * 2
            for u in range(2):
                tab[h, m + u] = table_one(h, m + u)
            return carry

        lax.fori_loop(low // 2, high // 2, step, 0)

    def lookups(low, high):
        def step(t, carry):
            h, b = t // 32, lax.rem(t, 32)
            sums = []
            at = pl.ds(pl.multiple_of(b * 8, 8), 8)
            for m in range(32):
                code = jnp.broadcast_to(codes[b, h, m : m + 1, :], (8, 128))
                index = code & 127
                first = lookup(tab[h, m, at, :128], index)
                second = lookup(tab[h, m, at, 128:], index)
                sums.append(jnp.where(code > 127, second, first))
            while len(sums) > 1:
                sums = [a + c for a, c in zip(sums[::2], sums[1::2])]
            acc[pl.ds(pl.multiple_of(t * 8, 8), 8), :] = sums[0]
            return carry

        lax.fori_loop(low, high, step, 0)

    def finish_estimates(h):
        rows = []
        for bb in range(4):
            base = (h * 32 + bb * 8) * 8
            off = valid[bb * 8 : bb * 8 + 8, :]
            parts = [acc[pl.ds(base + g, 8, stride=8), :] + off for g in range(8)]
            top = functools.reduce(jnp.maximum, parts)
            top = lane_reduce(top, lane, jnp.maximum)
            mass = functools.reduce(jnp.add, [jnp.where(off == 0.0, jnp.exp(a - top), 0.0) for a in parts])
            mass = lane_reduce(mass, lane, jnp.add)
            rows.append(top + jnp.log(mass))
        rows = jnp.concatenate(rows, axis=0)
        pick = jnp.where(iota((8, 128), 1) == iota((8, 128), 0) * 16, 1.0, 0.0)
        est_ref[h] = lax.dot_general(
            pick, rows, (((1,), (1,)), ((), ())), precision=lax.Precision.HIGHEST, preferred_element_type=F32
        )

    def merge(sources):
        stats = [a[8].astype(F32) for a in sources]
        top = functools.reduce(jnp.maximum, stats)
        scales = [jnp.exp(a - top) for a in stats]
        total = functools.reduce(
            jnp.add, [(pltpu.roll(a, 112, 1) + pltpu.roll(a, 96, 1)) * e for a, e in zip(stats, scales)]
        )
        sums = [
            functools.reduce(jnp.add, [e[:, n : n + 1] * a[n].astype(F32) for a, e in zip(sources, scales)])
            for n in range(8)
        ]
        return top, total, sums

    loads[3].wait()
    loads[4].wait()
    q2[0] = q[:, :8, :].reshape(256, 128)
    q2[1] = q[:, 8:, :].reshape(256, 128)
    tables(0, GAP1)

    for n in range(1, 8):
        copy1(n).wait_recv()
    top, total, sums = merge([send1.at[i]] + [recv1.at[n] for n in range(1, 8)])
    total_hi = total.astype(BF16).astype(F32)
    stat = jnp.where(lane < 8, top, jnp.where(
        lane < 32, pltpu.roll(total_hi, 16, 1), pltpu.roll(total - total_hi, 32, 1)))
    for n in range(8):
        send2[n] = sums[n].astype(BF16)
    send2[8] = stat.astype(BF16)

    def copy2(n):
        to = lax.rem(z + n, 8)
        return pltpu.make_async_remote_copy(
            send2, recv2.at[n], s2.at[n], r2.at[n], device_id=(to * 8 + i, x), device_id_type=MESH
        )

    for n in (4, 3, 5, 2, 6, 1, 7):
        copy2(n).start()
    tables(GAP1, 64)
    lookups(0, GAP2)

    for n in range(1, 8):
        copy2(n).wait_recv()
    top, total, sums = merge([send2] + [recv2.at[n] for n in range(1, 8)])
    for n in range(8):
        gath[i, n] = (sums[n] / total[:, n : n + 1]).astype(BF16)

    def copy4(n):
        to = lax.rem(i + n, 8)
        return pltpu.make_async_remote_copy(
            gath.at[i], gath.at[i], s4.at[n], r4.at[n], device_id=(z * 8 + to, x), device_id_type=MESH
        )

    def arrived4(n):
        slot = gath.at[lax.rem(i + 8 - n, 8)]
        return pltpu.make_async_remote_copy(
            slot, slot, s4.at[n], r4.at[n], device_id=(seq, x), device_id_type=MESH
        )

    for n in (4, 3, 5, 2, 6, 1, 7):
        copy4(n).start()
    att_ref[...] = gath[i, z]
    lookups(GAP2, 64)
    finish_estimates(0)
    loads[5].wait()
    for n in range(1, 8):
        arrived4(n).wait_recv()

    for n in range(8):
        g32[pl.ds(n * 64, 64), :] = gath[n].astype(F32).reshape(64, 128)
    products = []
    for h in range(2):
        columns = []
        for g in range(8):
            columns.append(jnp.concatenate(
                [g32[pl.ds((2 * y_ + h) * 64 + g, 8, stride=8), :] for y_ in range(4)], axis=0
            ).astype(BF16))
        products.append(jnp.dot(
            jnp.concatenate(columns, axis=1), w[pl.ds(h * 1024, 1024), :], preferred_element_type=F32
        ))
    product = products[0] + products[1]
    for y_ in range(4):
        part[pl.ds(y_, 8, stride=4), :] = product[y_ * 8 : y_ * 8 + 8]

    def copy5(n):
        to = lax.rem(x + n, 4)
        return pltpu.make_async_remote_copy(
            part.at[pl.ds(pl.multiple_of(to * 8, 8), 8), :], recv5.at[n], s5.at[n], r5.at[n],
            device_id=(seq, to), device_id_type=MESH,
        )

    for n in (2, 1, 3):
        copy5(n).start()
    finish_estimates(1)
    result = part[pl.ds(pl.multiple_of(x * 8, 8), 8), :]
    for n in range(1, 4):
        copy5(n).wait_recv()
        result = result + recv5[n]
    lay_ref[...] = result.astype(BF16)

    for n in range(1, 8):
        copy1(n).wait_send()
        copy2(n).wait_send()
        copy4(n).wait_send()
    for n in range(1, 4):
        copy5(n).wait_send()


def shards(queries, keys, values, codes, centroids, picks, block_len, out_weight):
    vmem = pltpu.VMEM
    dma = pltpu.SemaphoreType.DMA
    est, att, lay = pl.pallas_call(
        kernel,
        out_shape=(
            jax.ShapeDtypeStruct((2, 8, 32), F32),
            jax.ShapeDtypeStruct((8, 128), BF16),
            jax.ShapeDtypeStruct((8, 128), BF16),
        ),
        in_specs=[pl.BlockSpec(memory_space=pltpu.HBM)] * 8,
        out_specs=[pl.BlockSpec(memory_space=vmem)] * 3,
        scratch_shapes=[
            vmem((32, 16, 128), BF16),
            vmem((32, 2, 128, 128), BF16),
            vmem((32, 2, 128, 128), BF16),
            vmem((32, 2, 32, 128), jnp.int32),
            vmem((2, 4, 32, 256), F32),
            vmem((64, 64), jnp.int32),
            vmem((8, 32), jnp.int32),
            vmem((2048, 128), BF16),
            vmem((2, 32, 128), F32),
            vmem((32, 128), F32),
            vmem((2, 256, 128), BF16),
            vmem((2, 32, 256, 256), F32),
            vmem((512, 128), F32),
            vmem((32, 2, 8, 128), F32),
            vmem((32, 32, 128), F32),
            vmem((8, 9, 8, 128), BF16),
            vmem((8, 9, 8, 128), BF16),
            vmem((9, 8, 128), BF16),
            vmem((8, 9, 8, 128), BF16),
            vmem((8, 8, 8, 128), BF16),
            vmem((512, 128), F32),
            vmem((32, 128), F32),
            vmem((4, 8, 128), F32),
            dma((6,)), dma((4,)), dma((4,)),
            dma((8,)), dma((8,)), dma((8,)), dma((8,)), dma((8,)), dma((8,)), dma((4,)), dma((4,)),
        ],
        compiler_params=pltpu.CompilerParams(
            collective_id=0, has_side_effects=True, vmem_limit_bytes=67_043_328
        ),
        name="decode",
    )(
        queries,
        keys,
        values,
        codes,
        centroids,
        picks.reshape(64, 64),
        block_len.T,
        out_weight,
    )
    return est.transpose(2, 0, 1), att.reshape(1, 1, 1024), lay


def solution(mesh):
    placed = (
        P(None, "head", None),
        P(None, "head", "seq", None),
        P(None, "head", "seq", None),
        P(None, "head", None, "seq"),
        P("head", None, None, None),
        P(None, "head", None),
        P(None, "seq"),
        P("head", "seq"),
    )
    return jax.shard_map(
        shards,
        mesh=mesh,
        in_specs=placed,
        out_specs=(P(None, "head", "seq"), P("seq", "head", None), P("head", "seq")),
        check_vma=False,
    )
```

time: 68.6 us -> 43.2 us (0.63)
  Pallas kernels: 57 us -> 38.6 us
  local copies, waits for them, and re-layouts: 10.5 us -> 3.79 us
    pallas_call x1, Pallas kernels: 57 us -> 38.6 us  [shards(): pl.pallas_call(kernel, out_shape=(jax.ShapeDtypeStruct((2, 8, 32), F32),...]
    unnamed x18 -> x2, local copies, waits for them, and re-layouts: 9.91 us -> 2.54 us
where the time goes in v2:
time: 43.2 us; the launch traced here: 43 us
  Pallas kernels  38.6 us (89%)
  local copies, waits for them, and re-layouts  3.79 us (9%)
  between operations  0.64 us (1%)
    pallas_call x1, Pallas kernels, shards(): pl.pallas_call(kernel, out_shape=(jax.ShapeDtypeStruct((2, 8, 32), F32),...  38.6 us
    unnamed x2, local copies, waits for them, and re-layouts  2.54 us
    reshape x1, local copies, waits for them, and re-layouts, shards(): return (est.transpose(2, 0, 1), att.reshape(1, 1, 1024), lay)  1.25 us

profile of v2, /device:TPU:1, one launch (start us, length us, event | category | flops | bytes accessed | tf_op | source)
XLA Modules:
  0.0 43.0 jit_solution(15257816356906922102)
XLA Ops:
  0.6 38.6 %decode.1 = (f32[2,8,32]{2,1,0:T(8,128)}, bf16[8,128]{1,0:T(8,128)(2,1)}, bf16[8,128]{1,0:T(8,128)(2,1)}) custom-call(bf16[32,16,128]{2,1,0:T(8,128)(2,1)} %q_hbm.1, bf16[32,2,128,128]{3,2,1,0:T(8,128)(2,1)} %k_hbm.1, bf16[32,2,128,128]{3,2,1,0:T(8,128)(2,1)} %v_hbm.1, s32[32,2,32,128]{3,2,1,0:T(8,128)} %codes_hbm.1, f32[2,4,32,256]{3,2,1,0:T(8,128)} %cent_hbm.1, ...), custom_call_target="tpu_custom_call" | custom-call | tf_op jit(solution)/shard_map/decode/pallas_call | solution.py:317
  39.2 1.3 %reshape.13 = bf16[1,1,1024]{2,1,0:T(2,128)(2,1)} reshape(bf16[8,128]{1,0:T(8,128)(2,1)} %get-tuple-element.7) | data formatting | bytes 4096 | tf_op jit(solution)/shard_map/reshape | solution.py:367
  40.5 1.3 %copy.13 = f32[32,2,8]{0,2,1:T(8,128)} copy(f32[32,2,8]{0,2,1:T(8,128)} %bitcast.4) | data formatting | bytes 4096
  41.8 1.2 %copy.14 = bf16[8,128]{1,0:T(8,128)(2,1)} copy(bf16[8,128]{1,0:T(8,128)(2,1)} %get-tuple-element.14) | data formatting | bytes 4096

commit v3 on v2

--- a/solution.py
+++ b/solution.py
@@ -13,7 +13,8 @@
 F32 = jnp.float32
 BF16 = jnp.bfloat16
 SCALE = 128 ** -0.5
-GAP1 = 32
+STEP = 1280.0
+GAP1 = 16
 GAP2 = 32
 
 
@@ -147,42 +148,52 @@
     for n in (4, 3, 5, 2, 6, 1, 7):
         copy1(n).start()
 
-    def table_one(h, m):
-        row = iota((16, 256), 0) & 3
-        pattern = jnp.broadcast_to(cent[h, 3, pl.ds(m, 1), :], (16, 256))
-        for s in range(3):
-            pattern = jnp.where(row == s, cent[h, s, pl.ds(m, 1), :], pattern)
-        pattern = pattern * SCALE
-        hi = pattern.astype(BF16)
-        lo = (pattern - hi.astype(F32)).astype(BF16)
-        own = jnp.where(iota((16, 128), 1) // 4 == m, 1.0, 0.0).astype(BF16)
-        lhs = q2[h] * jnp.concatenate([own] * 16, axis=0)
-        rhs = jnp.concatenate([hi] * 8 + [lo] * 8, axis=0)
-        return jnp.dot(jnp.concatenate([lhs, lhs], axis=1), rhs, preferred_element_type=F32)
+    sub = iota((8, 128), 0)
 
     def tables(low, high):
         def step(t, carry):
-            h, m = t // 16, lax.rem(t, 16) * 2
-            for u in range(2):
-                tab[h, m + u] = table_one(h, m + u)
+            h, m = t // 16, lax.rem(t, 16)
+            row = iota((16, 256), 0)
+            tiles = []
+            for at in (m, m + 16):
+                pattern = jnp.broadcast_to(cent[h, 3, pl.ds(at, 1), :], (16, 256))
+                for s in range(3):
+                    pattern = jnp.where((row & 3) == s, cent[h, s, pl.ds(at, 1), :], pattern)
+                pattern = pattern * (SCALE * STEP)
+                hi = pattern.astype(BF16)
+                tiles.append((hi, (pattern - hi.astype(F32)).astype(BF16)))
+            rhs = jnp.concatenate(
+                [tiles[0][0]] * 4 + [tiles[1][0]] * 4 + [tiles[0][1]] * 4 + [tiles[1][1]] * 4, axis=0
+            )
+            target = jnp.where((row[:, :128] & 7) < 4, m, m + 16)
+            own = jnp.where(iota((16, 128), 1) // 4 == target, 1.0, 0.0).astype(BF16)
+            lhs = q2[h] * jnp.concatenate([own] * 32, axis=0)
+            table = jnp.dot(jnp.concatenate([lhs, lhs], axis=1), rhs, preferred_element_type=F32)
+            for b in range(32):
+                first = (table[b * 16 : b * 16 + 8] + 32768.5).astype(jnp.int32)
+                second = (table[b * 16 + 8 : b * 16 + 16] + 32768.5).astype(jnp.int32)
+                tab[h, m, b] = first | (second << 16)
             return carry
 
-        lax.fori_loop(low // 2, high // 2, step, 0)
+        lax.fori_loop(low, high, step, 0)
 
     def lookups(low, high):
         def step(t, carry):
             h, b = t // 32, lax.rem(t, 32)
-            sums = []
-            at = pl.ds(pl.multiple_of(b * 8, 8), 8)
-            for m in range(32):
-                code = jnp.broadcast_to(codes[b, h, m : m + 1, :], (8, 128))
+            firsts, seconds = [], []
+            for m in range(16):
+                code = jnp.where(sub < 4, codes[b, h, m : m + 1, :], codes[b, h, m + 16 : m + 17, :])
                 index = code & 127
-                first = lookup(tab[h, m, at, :128], index)
-                second = lookup(tab[h, m, at, 128:], index)
-                sums.append(jnp.where(code > 127, second, first))
-            while len(sums) > 1:
-                sums = [a + c for a, c in zip(sums[::2], sums[1::2])]
-            acc[pl.ds(pl.multiple_of(t * 8, 8), 8), :] = sums[0]
+                word = jnp.where(
+                    code > 127, lookup(tab[h, m, b, :, 128:], index), lookup(tab[h, m, b, :, :128], index)
+                )
+                firsts.append(word & 65535)
+                seconds.append(lax.shift_right_logical(word, 16))
+            at = pl.multiple_of(t * 16, 16)
+            for sums, rows in ((firsts, pl.ds(at, 8)), (seconds, pl.ds(at + 8, 8))):
+                while len(sums) > 1:
+                    sums = [a + c for a, c in zip(sums[::2], sums[1::2])]
+                acc[rows, :] = sums[0]
             return carry
 
         lax.fori_loop(low, high, step, 0)
@@ -190,9 +201,13 @@
     def finish_estimates(h):
         rows = []
         for bb in range(4):
-            base = (h * 32 + bb * 8) * 8
+            base = (h * 32 + bb * 8) * 16
             off = valid[bb * 8 : bb * 8 + 8, :]
-            parts = [acc[pl.ds(base + g, 8, stride=8), :] + off for g in range(8)]
+            parts = []
+            for g in range(8):
+                at = base + g // 4 * 8 + g % 4
+                total = acc[pl.ds(at, 8, stride=16), :] + acc[pl.ds(at + 4, 8, stride=16), :]
+                parts.append((total - 32 * 32768).astype(F32) * (1.0 / STEP) + off)
             top = functools.reduce(jnp.maximum, parts)
             top = lane_reduce(top, lane, jnp.maximum)
             mass = functools.reduce(jnp.add, [jnp.where(off == 0.0, jnp.exp(a - top), 0.0) for a in parts])
@@ -219,8 +234,14 @@
 
     loads[3].wait()
     loads[4].wait()
-    q2[0] = q[:, :8, :].reshape(256, 128)
-    q2[1] = q[:, 8:, :].reshape(256, 128)
+    low_half = iota((32, 8, 128), 1) < 4
+    for h in range(2):
+        own = q[...].astype(F32)[:, h * 8 : h * 8 + 8, :]
+        swapped = pltpu.roll(own, 4, 1)
+        both = jnp.concatenate(
+            [jnp.where(low_half, own, swapped), jnp.where(low_half, swapped, own)], axis=1
+        )
+        q2[h] = both.astype(BF16).reshape(512, 128)
     tables(0, GAP1)
 
     for n in range(1, 8):
@@ -241,7 +262,7 @@
 
     for n in (4, 3, 5, 2, 6, 1, 7):
         copy2(n).start()
-    tables(GAP1, 64)
+    tables(GAP1, 32)
     lookups(0, GAP2)
 
     for n in range(1, 8):
@@ -334,9 +355,9 @@
             vmem((2048, 128), BF16),
             vmem((2, 32, 128), F32),
             vmem((32, 128), F32),
-            vmem((2, 256, 128), BF16),
-            vmem((2, 32, 256, 256), F32),
-            vmem((512, 128), F32),
+            vmem((2, 512, 128), BF16),
+            vmem((2, 16, 32, 8, 256), jnp.int32),
+            vmem((1024, 128), jnp.int32),
             vmem((32, 2, 8, 128), F32),
             vmem((32, 32, 128), F32),
             vmem((8, 9, 8, 128), BF16),

time: 43.2 us -> 38.3 us (0.89)
  Pallas kernels: 38.6 us -> 33.6 us
    pallas_call x1, Pallas kernels: 38.6 us -> 33.6 us  [shards(): pl.pallas_call(kernel, out_shape=(jax.ShapeDtypeStruct((2, 8, 32), F32),...]
where the time goes in v3:
time: 38.3 us; the launch traced here: 38.1 us
  Pallas kernels  33.6 us (88%)
  local copies, waits for them, and re-layouts  3.79 us (10%)
  between operations  0.64 us (2%)
    pallas_call x1, Pallas kernels, shards(): pl.pallas_call(kernel, out_shape=(jax.ShapeDtypeStruct((2, 8, 32), F32),...  33.6 us
    unnamed x2, local copies, waits for them, and re-layouts  2.54 us
    reshape x1, local copies, waits for them, and re-layouts, shards(): return (est.transpose(2, 0, 1), att.reshape(1, 1, 1024), lay)  1.25 us

profile of v3, /device:TPU:1, one launch (start us, length us, event | category | flops | bytes accessed | tf_op | source)
XLA Modules:
  0.0 38.1 jit_solution(5464296979776122505)
XLA Ops:
  0.6 33.6 %decode.1 = (f32[2,8,32]{2,1,0:T(8,128)}, bf16[8,128]{1,0:T(8,128)(2,1)}, bf16[8,128]{1,0:T(8,128)(2,1)}) custom-call(bf16[32,16,128]{2,1,0:T(8,128)(2,1)} %q_hbm.1, bf16[32,2,128,128]{3,2,1,0:T(8,128)(2,1)} %k_hbm.1, bf16[32,2,128,128]{3,2,1,0:T(8,128)(2,1)} %v_hbm.1, s32[32,2,32,128]{3,2,1,0:T(8,128)} %codes_hbm.1, f32[2,4,32,256]{3,2,1,0:T(8,128)} %cent_hbm.1, ...), custom_call_target="tpu_custom_call" | custom-call | tf_op jit(solution)/shard_map/decode/pallas_call | solution.py:338
  34.3 1.3 %reshape.13 = bf16[1,1,1024]{2,1,0:T(2,128)(2,1)} reshape(bf16[8,128]{1,0:T(8,128)(2,1)} %get-tuple-element.7) | data formatting | bytes 4096 | tf_op jit(solution)/shard_map/reshape | solution.py:388
  35.5 1.3 %copy.13 = f32[32,2,8]{0,2,1:T(8,128)} copy(f32[32,2,8]{0,2,1:T(8,128)} %bitcast.4) | data formatting | bytes 4096
  36.8 1.2 %copy.14 = bf16[8,128]{1,0:T(8,128)(2,1)} copy(bf16[8,128]{1,0:T(8,128)(2,1)} %get-tuple-element.14) | data formatting | bytes 4096
